TPU v7x, 32 devices: a whole 2x2x4 slice. The times are simulated.
32 devices in a mesh: dp: 4 (over y, core), tm: 8 (over z, x).
Axes of the slice: x: 2, y: 2, z: 4, core: 2. Of those that a mesh axis runs over, the one named last changes fastest.
Arguments:
- latents: bfloat16 [4, 64, 64, 1280], P('dp', 'tm'), may hold values from -6 to 6
- conv_weight: bfloat16 [1280, 3840], replicated, may hold values from -0.09375 to 0.09375
- qkv_weight: bfloat16 [1280, 1920], replicated, may hold values from -2 to 2
- out_weight: bfloat16 [640, 1280], replicated, may hold values from -0.25 to 0.25
- out_cotangent: bfloat16 [4, 32, 64, 1280], P('dp', 'tm'), may hold values from -6 to 6
Outputs:
- input_grad: bfloat16 [4, 64, 64, 1280], P('dp', 'tm')
- conv_grad: bfloat16 [1280, 3840], P('tm')
- qkv_grad: bfloat16 [1280, 1920], P('tm')
- proj_grad: bfloat16 [640, 1280], P('tm')
All inputs are finite; a program needn't handle non-finite values.
Results may differ from a plain program's by a relative error of at most 0.04.
Values may be sent and summed in bfloat16 or wider, within the bound.
A program may use at most 192 MiB of HBM per device.

v0:
```python
import math
import jax
import jax.numpy as jnp
from jax import lax
from jax.sharding import PartitionSpec as P

HEADS = 10
HEAD = 64
EPSILON = 1e-05


def from_behind(shard, axis, by):
    devices = lax.axis_size(axis)
    pairs = [(i, i + by) for i in range(devices) if 0 <= i + by < devices]
    return lax.ppermute(shard, axis, pairs)


def dot_rows(left_side, right_side):
    return jnp.dot(left_side, right_side, preferred_element_type=jnp.float32)


def column_term(lefts, right_side):
    pieces = [
        lax.dot_general(
            operand, right_side, (((0,), (0,)), ((), ())), preferred_element_type=jnp.float32
        )
        for operand in lefts
    ]
    return jnp.concatenate(pieces, axis=1)


def head_shape(packed):
    return packed.shape[:3] + (HEADS, HEAD)


def attend_forward(qkv_loc):
    width = qkv_loc.shape[-1] // 3
    shape = head_shape(qkv_loc)
    queries = qkv_loc[..., :width].reshape(shape)
    keys = qkv_loc[..., width : 2 * width].reshape(shape)
    values = qkv_loc[..., 2 * width :].reshape(shape)
    scores = jnp.einsum(
        "vqlhd,vklhd->vlhqk", queries, keys, preferred_element_type=jnp.float32
    ) / math.sqrt(HEAD)
    highest = jnp.max(scores, axis=-1, keepdims=True)
    expo = jnp.exp(scores - highest)
    probs = expo / jnp.sum(expo, axis=-1, keepdims=True)
    probs_b = probs.astype(jnp.bfloat16)
    attended = jnp.einsum(
        "vlhqk,vklhd->vqlhd", probs_b, values, preferred_element_type=jnp.float32
    ).astype(jnp.bfloat16)
    return (attended.reshape(qkv_loc.shape[:3] + (width,)), probs, probs_b)


def attend_backward(qkv_loc, attended, probs, probs_b, grad_att):
    width = qkv_loc.shape[-1] // 3
    shape = head_shape(qkv_loc)
    queries = qkv_loc[..., :width].reshape(shape)
    keys = qkv_loc[..., width : 2 * width].reshape(shape)
    values = qkv_loc[..., 2 * width :].reshape(shape)
    grad_heads = grad_att.reshape(shape)
    grad_values = jnp.einsum(
        "vlhqk,vqlhd->vklhd", probs_b, grad_heads, preferred_element_type=jnp.float32
    ).astype(jnp.bfloat16)
    grad_probs = jnp.einsum(
        "vqlhd,vklhd->vlhqk", grad_heads, values, preferred_element_type=jnp.float32
    )
    row_delta = jnp.sum(
        grad_heads.astype(jnp.float32) * attended.reshape(shape).astype(jnp.float32), axis=-1
    )
    row_delta = jnp.transpose(row_delta, (0, 2, 3, 1))[..., None]
    grad_scores = (probs * (grad_probs - row_delta) / math.sqrt(HEAD)).astype(jnp.bfloat16)
    grad_queries = jnp.einsum(
        "vlhqk,vklhd->vqlhd", grad_scores, keys, preferred_element_type=jnp.float32
    ).astype(jnp.bfloat16)
    grad_keys = jnp.einsum(
        "vlhqk,vqlhd->vklhd", grad_scores, queries, preferred_element_type=jnp.float32
    ).astype(jnp.bfloat16)
    flat_shape = qkv_loc.shape[:3] + (width,)
    return jnp.concatenate(
        [
            grad_queries.reshape(flat_shape),
            grad_keys.reshape(flat_shape),
            grad_values.reshape(flat_shape),
        ],
        axis=-1,
    )


def local(latents, conv_weight, qkv_weight, out_weight, out_cotangent):
    videos, frames, places, width = latents.shape
    half = frames // 2
    attn_width = out_weight.shape[0]
    split = latents.reshape(videos, half, 2, places, width)
    even_frames = split[:, :, 0]
    odd_frames = split[:, :, 1]
    rim_input = from_behind(odd_frames[:, half - 1 :], "tm", 1)
    prev_frames = jnp.concatenate([rim_input, odd_frames[:, : half - 1]], axis=1)
    local_rows = videos * half * places

    def as_rows(values):
        return values.reshape(local_rows, values.shape[-1])

    tap_zero = conv_weight[:, :width]
    tap_one = conv_weight[:, width : 2 * width]
    tap_two = conv_weight[:, 2 * width :]
    prev_rows = as_rows(prev_frames)
    even_rows = as_rows(even_frames)
    odd_rows = as_rows(odd_frames)
    hidden = (
        dot_rows(prev_rows, tap_zero) + dot_rows(even_rows, tap_one) + dot_rows(odd_rows, tap_two)
    ).astype(jnp.bfloat16)
    hidden_f = hidden.astype(jnp.float32)
    centred = hidden_f - jnp.mean(hidden_f, axis=-1, keepdims=True)
    inv_std = lax.rsqrt(jnp.mean(centred * centred, axis=-1, keepdims=True) + EPSILON)
    unit_rows = centred * inv_std
    normed = unit_rows.astype(jnp.bfloat16)
    qkv_rows = (
        dot_rows(normed, qkv_weight)
        .astype(jnp.bfloat16)
        .reshape(videos, half, places, 3 * attn_width)
    )
    qkv_loc = lax.all_to_all(qkv_rows, "tm", split_axis=2, concat_axis=1, tiled=True)
    attended, probs, probs_b = attend_forward(qkv_loc)
    cotangent_rows = as_rows(out_cotangent)
    attended_time = lax.all_to_all(attended, "tm", split_axis=1, concat_axis=2, tiled=True)
    grad_time = (
        dot_rows(cotangent_rows, out_weight.T)
        .astype(jnp.bfloat16)
        .reshape(videos, half, places, attn_width)
    )
    grad_att = lax.all_to_all(grad_time, "tm", split_axis=2, concat_axis=1, tiled=True)
    proj_left = as_rows(attended_time)
    grad_qkv_loc = attend_backward(qkv_loc, attended, probs, probs_b, grad_att)
    grad_qkv = as_rows(lax.all_to_all(grad_qkv_loc, "tm", split_axis=1, concat_axis=2, tiled=True))
    grad_normed = dot_rows(grad_qkv, qkv_weight.T)
    correction = (
        grad_normed
        - jnp.mean(grad_normed, axis=-1, keepdims=True)
        - unit_rows * jnp.mean(grad_normed * unit_rows, axis=-1, keepdims=True)
    )
    grad_hidden = (cotangent_rows.astype(jnp.float32) + inv_std * correction).astype(jnp.bfloat16)
    grad_four = grad_hidden.reshape(videos, half, places, width)
    rim_after = from_behind(grad_four[:, :1], "tm", -1)
    grad_next = jnp.concatenate([grad_four[:, 1:], rim_after], axis=1)
    grad_even = dot_rows(grad_hidden, tap_one.T).astype(jnp.bfloat16)
    grad_odd = (dot_rows(grad_hidden, tap_two.T) + dot_rows(as_rows(grad_next), tap_zero.T)).astype(
        jnp.bfloat16
    )
    input_grad = jnp.stack(
        [
            grad_even.reshape(videos, half, places, width),
            grad_odd.reshape(videos, half, places, width),
        ],
        axis=2,
    ).reshape(latents.shape)
    dp_count = lax.axis_size("dp")
    tm_count = lax.axis_size("tm")
    grad_scale = 1.0 / math.sqrt(dp_count * tm_count * local_rows)
    conv_part = lax.psum_scatter(
        column_term((prev_rows, even_rows, odd_rows), grad_hidden).astype(jnp.bfloat16),
        "tm",
        scatter_dimension=0,
        tiled=True,
    )
    qkv_part = lax.psum_scatter(
        column_term((normed,), grad_qkv).astype(jnp.bfloat16), "tm", scatter_dimension=0, tiled=True
    )
    proj_part = lax.psum_scatter(
        column_term((proj_left,), cotangent_rows).astype(jnp.bfloat16),
        "tm",
        scatter_dimension=0,
        tiled=True,
    )
    conv_total, qkv_total, proj_total = (
        lax.psum(conv_part, "dp").astype(jnp.float32),
        lax.psum(qkv_part, "dp").astype(jnp.float32),
        lax.psum(proj_part, "dp").astype(jnp.float32),
    )
    conv_grad = (conv_total * grad_scale).astype(jnp.bfloat16)
    qkv_grad = (qkv_total * grad_scale).astype(jnp.bfloat16)
    proj_grad = (proj_total * grad_scale).astype(jnp.bfloat16)
    return (input_grad, conv_grad, qkv_grad, proj_grad)


def solution(mesh):
    return jax.shard_map(
        local,
        mesh=mesh,
        in_specs=(P("dp", "tm", None, None), P(), P(), P(), P("dp", "tm", None, None)),
        out_specs=(P("dp", "tm", None, None), P("tm", None), P("tm", None), P("tm", None)),
        check_vma=False,
    )
```

profile of v0, /device:TPU:0, one launch (start us, length us, event | category | flops | bytes accessed | tf_op | source)
XLA Modules:
  0.0 576.1 jit_solution(3840173619625434894)
XLA Ops:
  8.6 1.8 convolution_convert_fusion.10
  11.4 7.3 %all-to-all-start.1 = ((bf16[1,4,64,640]{3,1,0,2:T(4,128)(2,1)}), bf16[1,4,64,640]{3,1,0,2:T(4,128)(2,1)S(1)}, u32[]{:S(2)}, u32[]{:S(2)}) async-start(bf16[1,4,64,640]{3,1,0,2:T(4,128)(2,1)} %copy.89), calls=%async_computation.1 | async-start | bytes 655360 | tf_op jit(solution)/shard_map/all_to_all | solution.py:132
  18.9 4.2 collective-permute-start
  23.0 2.9 fusion.5
  31.2 1.7 copy.84
  32.9 8.1 %all-to-all-start = ((bf16[1,4,64,1920]{3,1,0,2:T(4,128)(2,1)}), bf16[1,4,64,1920]{3,1,0,2:T(4,128)(2,1)}, u32[]{:S(2)}, u32[]{:S(2)}) async-start(bf16[1,4,64,1920]{3,1,0,2:T(4,128)(2,1)} %copy.84), calls=%async_computation | async-start | bytes 1966080 | tf_op jit(solution)/shard_map/all_to_all | solution.py:123
  42.9 1.8 reshape.177
  44.7 21.2 %all-to-all-done = bf16[1,4,64,1920]{3,1,0,2:T(4,128)(2,1)} async-done(((bf16[1,4,64,1920]{3,1,0,2:T(4,128)(2,1)}), bf16[1,4,64,1920]{3,1,0,2:T(4,128)(2,1)}, u32[]{:S(2)}, u32[]{:S(2)}) %all-to-all-start) | async-done | bytes 983072 | tf_op jit(solution)/shard_map/all_to_all | solution.py:123
  72.0 3.7 fusion.74
  75.7 3.2 fusion.45
  78.9 2.1 fusion.41
  85.4 1.8 reshape.168
  88.6 1.8 reshape.169
  90.4 2.4 copy.105
  92.8 1.8 reshape.170
  94.7 27.3 %all_to_all.63 = bf16[1,32,8,1920]{3,2,0,1:T(8,128)(2,1)S(1)} all-to-all(bf16[1,32,8,1920]{3,2,0,1:T(8,128)(2,1)S(1)} %maximum_bitcast_fusion), channel_id=1, replica_groups=mesh['dp'=4,'tm'=8] {'tm'}, dimensions={1} | all-to-all | bytes 1966080 | tf_op jit(solution)/shard_map/all_to_all | solution.py:135
  122.2 4.5 fusion.71
  131.0 4.4 pad_maximum_fusion
  135.5 13.7 %copy.116 = bf16[1280,3840]{1,0:T(8,128)(2,1)} copy(bf16[1280,3840]{0,1:T(8,128)(2,1)} %pad_maximum_fusion) | data formatting | bytes 19660800
  151.3 22.2 %all_to_all.64 = bf16[1,32,8,640]{3,2,0,1:T(8,128)(2,1)S(1)} all-to-all(bf16[1,32,8,640]{3,2,0,1:T(8,128)(2,1)S(1)} %bitcast.115), channel_id=1, replica_groups=mesh['dp'=4,'tm'=8] {'tm'}, dimensions={1} | all-to-all | bytes 655360 | tf_op jit(solution)/shard_map/all_to_all | solution.py:126
  173.5 1.8 convolution_convert_fusion.4
  176.6 4.0 convolution_convert_fusion
  182.2 3.0 fusion.24
  185.2 140.9 %reduce-scatter.10.cloned.1.call-done = bf16[160,3840]{1,0:T(8,128)(2,1)} async-done(((bf16[1280,3840]{1,0:T(8,128)(2,1)}), bf16[160,3840]{1,0:T(8,128)(2,1)}) %reduce-scatter.10.cloned.1.call-update) | async-done | bytes 1228816
  326.1 3.6 copy.117
  329.7 64.3 %reduce-scatter.8.cloned.1.call-done = bf16[80,1280]{1,0:T(8,128)(2,1)} async-done(((bf16[640,1280]{1,0:T(8,128)(2,1)}), bf16[80,1280]{1,0:T(8,128)(2,1)}) %reduce-scatter.8.cloned.1.call-update) | async-done | bytes 204816 | tf_op jit(solution)/shard_map/reduce_scatter | solution.py:169
  394.0 101.7 %reduce-scatter.6.cloned.1.call-done = bf16[160,1920]{1,0:T(8,128)(2,1)} async-done(((bf16[1280,1920]{1,0:T(8,128)(2,1)}), bf16[160,1920]{1,0:T(8,128)(2,1)}) %reduce-scatter.6.cloned.1.call-update) | async-done | bytes 614416 | tf_op jit(solution)/shard_map/reduce_scatter | solution.py:166
  495.7 3.0 fusion.3
  498.8 3.0 fusion.27
  503.1 57.7 %all-reduce.3.cloned.1.call-done = (bf16[160,3840]{0,1:T(8,128)(2,1)}, bf16[160,1920]{1,0:T(8,128)(2,1)}, bf16[80,1280]{1,0:T(8,128)(2,1)}) async-done(((bf16[160,3840]{0,1:T(8,128)(2,1)}, bf16[160,1920]{1,0:T(8,128)(2,1)}, bf16[80,1280]{1,0:T(8,128)(2,1)}), (bf16[160,3840]{0,1:T(8,128)(2,1)}, bf16[160,1920]{1,0:T(8,128)(2,1)}, bf16[80,1280]{1,0:T(8,128)(2,1)})) %all-reduce.3.cloned.1.call-update) | async-done | bytes 2048016 | tf_op jit(solution)/shard_map/psum | solution.py:176
  560.8 3.2 multiply_convert_fusion
  564.1 3.8 copy.112
  (100 shorter events, 33.7 us)
Async XLA Ops:
  7.2 1.4 copy-start
  10.4 8.2 %copy-start.13 = (bf16[1,8,64,1280]{3,2,1,0:T(8,128)(2,1)S(1)}, bf16[1,8,64,1280]{3,2,1,0:T(8,128)(2,1)}, u32[]{:S(2)}) copy-start(bf16[1,8,64,1280]{3,2,1,0:T(8,128)(2,1)} %param.5) | copy-start | bytes 3932164
  11.4 21.5 %all-to-all-start.1 = ((bf16[1,4,64,640]{3,1,0,2:T(4,128)(2,1)}), bf16[1,4,64,640]{3,1,0,2:T(4,128)(2,1)S(1)}, u32[]{:S(2)}, u32[]{:S(2)}) async-start(bf16[1,4,64,640]{3,1,0,2:T(4,128)(2,1)} %copy.89), calls=%async_computation.1 | async-start | bytes 655360 | tf_op jit(solution)/shard_map/all_to_all | solution.py:132
  18.6 7.4 %copy-start.14 = (bf16[1280,3840]{1,0:T(8,128)(2,1)S(1)}, bf16[1280,3840]{1,0:T(8,128)(2,1)}, u32[]{:S(2)}) copy-start(bf16[1280,3840]{1,0:T(8,128)(2,1)} %param.6) | copy-start | bytes 29491204
  18.8 7.2 %copy-start.10 = (bf16[1,4,1,64,1280]{4,3,2,1,0:T(8,128)(2,1)}, bf16[1,4,1,64,1280]{4,3,2,1,0:T(8,128)(2,1)S(1)}, u32[]{:S(2)}) copy-start(bf16[1,4,1,64,1280]{4,3,2,1,0:T(8,128)(2,1)S(1)} %get-tuple-element.31) | copy-start | bytes 1966084
  18.8 7.2 %copy-start.8 = (bf16[1,4,1,64,1280]{4,3,2,1,0:T(8,128)(2,1)}, bf16[1,4,1,64,1280]{4,3,2,1,0:T(8,128)(2,1)S(1)}, u32[]{:S(2)}) copy-start(bf16[1,4,1,64,1280]{4,3,2,1,0:T(8,128)(2,1)S(1)} %get-tuple-element.30) | copy-start | bytes 1966084
  18.9 8.2 %collective-permute-start = (bf16[1,1,64,1280]{3,2,1,0:T(8,128)(2,1)S(1)}, bf16[1,1,64,1280]{3,2,1,0:T(8,128)(2,1)S(1)}, u32[]{:S(2)}, u32[]{:S(2)}) collective-permute-start(bf16[1,1,64,1280]{3,2,1,0:T(8,128)(2,1)S(1)} %slice.52), channel_id=1, source_target_pairs={{0,1},{1,2},{2,3},{3,4},{4,5},{5,6},{6,7},{8,9},{9,10},{10,11},{11... | collective-permute-start | bytes 491528 | tf_op jit(solution)/shard_map/ppermute | solution.py:15
  27.2 2.2 slice-start
  27.2 2.4 slice-start.1
  32.9 33.0 %all-to-all-start = ((bf16[1,4,64,1920]{3,1,0,2:T(4,128)(2,1)}), bf16[1,4,64,1920]{3,1,0,2:T(4,128)(2,1)}, u32[]{:S(2)}, u32[]{:S(2)}) async-start(bf16[1,4,64,1920]{3,1,0,2:T(4,128)(2,1)} %copy.84), calls=%async_computation | async-start | bytes 1966080 | tf_op jit(solution)/shard_map/all_to_all | solution.py:123
  41.0 285.2 %reduce-scatter.10.cloned.1.call-start = ((), (), s32[]{:S(2)}) async-start(), calls=%async_computation.9 | async-start | bytes 11059200
  75.7 3.2 copy-start.12
  75.7 3.2 copy-start.16
  75.7 3.2 copy-start.19
  78.9 2.1 copy-start.15
  81.0 1.2 copy-start.4
  82.3 1.2 copy-start.5
  122.2 4.5 copy-start.2
  122.2 4.5 copy-start.6
  126.7 1.1 copy-start.11
  127.8 1.1 copy-start.9
  149.2 244.8 %reduce-scatter.8.cloned.1.call-start = ((), (), s32[]{:S(2)}) async-start(), calls=%async_computation.8 | async-start | bytes 1843200 | tf_op jit(solution)/shard_map/reduce_scatter | solution.py:169
  151.3 22.2 %copy-start.7 = (bf16[1,4,64,1280]{3,2,1,0:T(8,128)(2,1)S(1)}, bf16[1,4,64,1280]{3,2,1,0:T(8,128)(2,1)}, u32[]{:S(2)}) copy-start(bf16[1,4,64,1280]{3,2,1,0:T(8,128)(2,1)} %param.9) | copy-start | bytes 1966084
  175.4 1.2 copy-start.3
  175.4 320.3 %reduce-scatter.6.cloned.1.call-start = ((), (), s32[]{:S(2)}) async-start(), calls=%async_computation.7 | async-start | bytes 5529600 | tf_op jit(solution)/shard_map/reduce_scatter | solution.py:166
  180.6 380.3 %all-reduce.3.cloned.1.call-start = ((), (), s32[]{:S(2)}) async-start(), calls=%async_computation.10 | async-start | bytes 5570560 | tf_op jit(solution)/shard_map/psum | solution.py:176
  180.6 318.1 %collective-permute-start.1 = (bf16[1,1,64,1280]{3,2,1,0:T(8,128)(2,1)S(1)}, bf16[1,1,64,1280]{3,2,1,0:T(8,128)(2,1)S(1)}, u32[]{:S(2)}, u32[]{:S(2)}) collective-permute-start(bf16[1,1,64,1280]{3,2,1,0:T(8,128)(2,1)S(1)} %slice.59), channel_id=1, source_target_pairs={{1,0},{2,1},{3,2},{4,3},{5,4},{6,5},{7,6},{9,8},{10,9},{11,10},{12... | collective-permute-start | bytes 491528 | tf_op jit(solution)/shard_map/ppermute | solution.py:15
  564.1 3.8 copy-start.18
  564.1 4.5 copy-start.17
  564.1 5.5 copy-start.1
Sparse Core Ops, SparseCore 0:
  149.3 176.7 reduce-scatter.9
  329.6 64.3 reduce-scatter.7
  398.1 97.5 reduce-scatter.5
  498.1 62.6 all-reduce.2
where the time goes:
time: 578 us; the launch traced here: 576 us
  waiting for transfers between devices  386 us (67%)
  local copies, waits for them, and re-layouts  52.3 us (9%)
  blocking collectives  49.5 us (9%)
  matrix products  42.2 us (7%)
  starting transfers between devices  21.4 us (4%)
  between operations  14.2 us (2%)
  other arithmetic  10.5 us (2%)
    unnamed x5, waiting for transfers between devices  141 us
    reduce_scatter x1, waiting for transfers between devices, local(): lax.psum_scatter(column_term((normed,), grad_qkv).astype(jnp.bfloat16), '...  102 us
    reduce_scatter x1, waiting for transfers between devices, local(): lax.psum_scatter(column_term((proj_left,), cotangent_rows).astype(jnp.bfl...  64.3 us
    psum x1, waiting for transfers between devices, local(): lax.psum(conv_part, 'dp').astype(jnp.float32)  57.7 us
    all_to_all x1, blocking collectives, local(): lax.all_to_all(grad_qkv_loc, 'tm', split_axis=1, concat_axis=2, tiled=True)  27.3 us
    unnamed x47, local copies, waits for them, and re-layouts  26.2 us
    all_to_all x1, blocking collectives, local(): lax.all_to_all(attended, 'tm', split_axis=1, concat_axis=2, tiled=True)  22.2 us
    dot_general x9, matrix products, dot_rows(): return jnp.dot(left_side, right_side, preferred_element_type=jnp.float32)  22 us
  transfers between devices with their start and end apart: 8, of which 5 were waited for; matrix products, arithmetic and copies ran while one was open for 6% of the time, Pallas kernels for 0%

commit v1 on v0

--- a/solution.py
+++ b/solution.py
@@ -173,7 +173,7 @@
         tiled=True,
     )
     conv_total, qkv_total, proj_total = (
-        lax.psum(conv_part, "dp").astype(jnp.float32),
+        lax.all_gather(conv_part, axis_name="dp").sum(axis=0).astype(jnp.float32),
         lax.psum(qkv_part, "dp").astype(jnp.float32),
         lax.psum(proj_part, "dp").astype(jnp.float32),
     )

time: 578 us -> 531 us (0.919)
  waiting for transfers between devices: 386 us -> 355 us
  blocking collectives: 49.5 us -> 33.4 us
  local copies, waits for them, and re-layouts: 52.3 us -> 41.7 us
  matrix products: 42.2 us -> 48.2 us
    reduce_scatter x0 -> x1, waiting for transfers between devices: none -> 172 us  [local(): lax.psum_scatter(column_term((prev_rows, even_rows, odd_rows), grad_hidde...]
    unnamed x5, waiting for transfers between devices: 141 us -> 0.08 us
    reduce_scatter x1, waiting for transfers between devices: 64.3 us -> 0.02 us  [local(): lax.psum_scatter(column_term((proj_left,), cotangent_rows).astype(jnp.bfl...]
    all_gather x0 -> x1, waiting for transfers between devices: none -> 36.5 us  [local(): lax.all_gather(conv_part, axis_name='dp').sum(axis=0).astype(jnp.float32)]
    psum x1, waiting for transfers between devices: 57.7 us -> 24.2 us  [local(): lax.psum(qkv_part, 'dp').astype(jnp.float32)]
    all_to_all x1 -> x0, blocking collectives: 22.2 us -> none  [local(): lax.all_to_all(attended, 'tm', split_axis=1, concat_axis=2, tiled=True)]
    unnamed x47 -> x31, local copies, waits for them, and re-layouts: 26.2 us -> 15.1 us
    all_to_all x0 -> x1, waiting for transfers between devices: none -> 7.25 us  [local(): lax.all_to_all(attended, 'tm', split_axis=1, concat_axis=2, tiled=True)]
  transfers between devices with their start and end apart: 8 -> 10, of which waited for: 5 -> 7; matrix products, arithmetic and copies ran while one was open for 6% -> 15% of each run, Pallas kernels for 0% -> 0%
where the time goes in v1:
time: 531 us; the launch traced here: 529 us
  waiting for transfers between devices  355 us (67%)
  matrix products  48.2 us (9%)
  local copies, waits for them, and re-layouts  41.7 us (8%)
  blocking collectives  33.4 us (6%)
  starting transfers between devices  21.1 us (4%)
  other arithmetic  15.9 us (3%)
  between operations  14.2 us (3%)
    reduce_scatter x1, waiting for transfers between devices, local(): lax.psum_scatter(column_term((prev_rows, even_rows, odd_rows), grad_hidde...  172 us
    reduce_scatter x1, waiting for transfers between devices, local(): lax.psum_scatter(column_term((normed,), grad_qkv).astype(jnp.bfloat16), '...  94.8 us
    all_gather x1, waiting for transfers between devices, local(): lax.all_gather(conv_part, axis_name='dp').sum(axis=0).astype(jnp.float32)  36.5 us
    all_to_all x1, blocking collectives, local(): lax.all_to_all(grad_qkv_loc, 'tm', split_axis=1, concat_axis=2, tiled=True)  33.4 us
    dot_general x9, matrix products, dot_rows(): return jnp.dot(left_side, right_side, preferred_element_type=jnp.float32)  24.6 us
    psum x1, waiting for transfers between devices, local(): lax.psum(qkv_part, 'dp').astype(jnp.float32)  24.2 us
    all_to_all x1, waiting for transfers between devices, local(): lax.all_to_all(qkv_rows, 'tm', split_axis=2, concat_axis=1, tiled=True)  19.1 us
    unnamed x31, local copies, waits for them, and re-layouts  15.1 us
  transfers between devices with their start and end apart: 10, of which 7 were waited for; matrix products, arithmetic and copies ran while one was open for 15% of the time, Pallas kernels for 0%

profile of v1, /device:TPU:0, one launch (start us, length us, event | category | flops | bytes accessed | tf_op | source)
XLA Modules:
  0.0 529.4 jit_solution(17005099139667355074)
XLA Ops:
  7.2 2.5 slice_bitcast_fusion
  10.4 4.8 collective-permute-start
  17.0 4.9 all-to-all-start.1
  21.9 3.0 fusion.5
  24.9 2.9 fusion.9
  28.0 3.2 fusion.73
  34.9 6.0 %all-to-all-start = ((bf16[1,4,64,1920]{3,1,0,2:T(4,128)(2,1)}), bf16[1,4,64,1920]{3,1,0,2:T(4,128)(2,1)S(1)}, u32[]{:S(2)}, u32[]{:S(2)}) async-start(bf16[1,4,64,1920]{3,1,0,2:T(4,128)(2,1)} %copy.83), calls=%async_computation | async-start | bytes 1966080 | tf_op jit(solution)/shard_map/all_to_all | solution.py:123
  42.8 2.7 reshape.177
  45.5 19.1 %all-to-all-done = bf16[1,4,64,1920]{3,1,0,2:T(4,128)(2,1)S(1)} async-done(((bf16[1,4,64,1920]{3,1,0,2:T(4,128)(2,1)}), bf16[1,4,64,1920]{3,1,0,2:T(4,128)(2,1)S(1)}, u32[]{:S(2)}, u32[]{:S(2)}) %all-to-all-start) | async-done | bytes 983072 | tf_op jit(solution)/shard_map/all_to_all | solution.py:123
  68.9 2.7 reshape.167
  71.6 3.4 fusion.74
  75.0 3.7 fusion.41
  80.4 3.4 all-to-all-start.3
  84.6 2.4 reshape.166
  87.0 7.2 %all-to-all-done.3 = bf16[1,32,8,640]{3,2,0,1:T(8,128)(2,1)S(1)} async-done(((bf16[1,32,8,640]{3,2,0,1:T(8,128)(2,1)}), bf16[1,32,8,640]{3,2,0,1:T(8,128)(2,1)S(1)}, u32[]{:S(2)}, u32[]{:S(2)}) %all-to-all-start.3) | async-done | bytes 327712 | tf_op jit(solution)/shard_map/all_to_all | solution.py:126
  97.4 2.8 fusion.40
  102.0 2.0 fusion.44
  105.6 2.2 fusion.45
  110.6 33.4 %all_to_all.63 = bf16[1,32,8,1920]{3,2,0,1:T(8,128)(2,1)S(1)} all-to-all(bf16[1,32,8,1920]{3,2,0,1:T(8,128)(2,1)S(1)} %maximum_bitcast_fusion), channel_id=1, replica_groups=mesh['dp'=4,'tm'=8] {'tm'}, dimensions={1} | all-to-all | bytes 1966080 | tf_op jit(solution)/shard_map/all_to_all | solution.py:135
  144.1 3.9 convolution_convert_fusion
  148.3 4.1 fusion.71
  156.3 4.4 pad_maximum_fusion
  160.7 13.7 %copy.115 = bf16[1280,3840]{1,0:T(8,128)(2,1)} copy(bf16[1280,3840]{0,1:T(8,128)(2,1)} %pad_maximum_fusion) | data formatting | bytes 19660800
  174.5 94.8 %reduce-scatter.6.cloned.1.call-done = bf16[160,1920]{1,0:T(8,128)(2,1)} async-done(((bf16[1280,1920]{1,0:T(8,128)(2,1)}), bf16[160,1920]{1,0:T(8,128)(2,1)}) %reduce-scatter.6.cloned.1.call-update) | async-done | bytes 614416 | tf_op jit(solution)/shard_map/reduce_scatter | solution.py:166
  269.3 172.3 %reduce-scatter.10.cloned.1.call-done = bf16[160,3840]{1,0:T(8,128)(2,1)} async-done(((bf16[1280,3840]{1,0:T(8,128)(2,1)}), bf16[160,3840]{1,0:T(8,128)(2,1)}) %reduce-scatter.10.cloned.1.call-update) | async-done | bytes 1228816 | tf_op jit(solution)/shard_map/reduce_scatter | solution.py:160
  443.0 3.0 fusion.24
  446.0 3.0 fusion.3
  449.6 3.0 fusion.27
  453.9 24.2 %all-reduce.3.cloned.1.call-done = (bf16[160,1920]{1,0:T(8,128)(2,1)}, bf16[80,1280]{1,0:T(8,128)(2,1)}) async-done(((bf16[160,1920]{1,0:T(8,128)(2,1)}, bf16[80,1280]{1,0:T(8,128)(2,1)}), (bf16[160,1920]{1,0:T(8,128)(2,1)}, bf16[80,1280]{1,0:T(8,128)(2,1)})) %all-reduce.3.cloned.1.call-update) | async-done | bytes 819216 | tf_op jit(solution)/shard_map/psum | solution.py:177
  479.8 2.0 multiply_convert_fusion.1
  481.7 36.5 %all-gather.3.cloned.1.call-done = bf16[640,3840]{1,0:T(8,128)(2,1)} async-done(((bf16[160,3840]{1,0:T(8,128)(2,1)}), bf16[640,3840]{1,0:T(8,128)(2,1)}) %all-gather.3.cloned.1.call-update) | async-done | bytes 4915216 | tf_op jit(solution)/shard_map/all_gather | solution.py:176
  518.3 3.4 reduce_sum.75
  (89 shorter events, 34.5 us)
Async XLA Ops:
  7.2 8.1 %copy-start = (bf16[640,1280]{1,0:T(8,128)(2,1)S(1)}, bf16[640,1280]{1,0:T(8,128)(2,1)}, u32[]{:S(2)}) copy-start(bf16[640,1280]{1,0:T(8,128)(2,1)} %param.8) | copy-start | bytes 4915204
  7.2 8.1 %copy-start.4 = (bf16[1,4,64,1280]{3,2,1,0:T(8,128)(2,1)S(1)}, bf16[1,4,64,1280]{3,2,1,0:T(8,128)(2,1)}, u32[]{:S(2)}) copy-start(bf16[1,4,64,1280]{3,2,1,0:T(8,128)(2,1)} %param.9) | copy-start | bytes 1966084
  9.7 12.2 %copy-start.8 = (bf16[1,4,1,64,1280]{4,3,2,1,0:T(8,128)(2,1)}, bf16[1,4,1,64,1280]{4,3,2,1,0:T(8,128)(2,1)S(1)}, u32[]{:S(2)}) copy-start(bf16[1,4,1,64,1280]{4,3,2,1,0:T(8,128)(2,1)S(1)} %get-tuple-element.10) | copy-start | bytes 1966084
  10.4 17.5 %collective-permute-start = (bf16[1,1,64,1280]{3,2,1,0:T(8,128)(2,1)}, bf16[1,1,64,1280]{3,2,1,0:T(8,128)(2,1)S(1)}, u32[]{:S(2)}, u32[]{:S(2)}) collective-permute-start(bf16[1,1,64,1280]{3,2,1,0:T(8,128)(2,1)} %slice.52), channel_id=1, source_target_pairs={{0,1},{1,2},{2,3},{3,4},{4,5},{5,6},{6,7},{8,9},{9,10},{10,11},{11... | collective-permute-start | bytes 491528 | tf_op jit(solution)/shard_map/ppermute | solution.py:15
  17.0 17.9 %all-to-all-start.1 = ((bf16[1,4,64,640]{3,1,0,2:T(4,128)(2,1)}), bf16[1,4,64,640]{3,1,0,2:T(4,128)(2,1)}, u32[]{:S(2)}, u32[]{:S(2)}) async-start(bf16[1,4,64,640]{3,1,0,2:T(4,128)(2,1)} %copy.88), calls=%async_computation.1 | async-start | bytes 655360 | tf_op jit(solution)/shard_map/all_to_all | solution.py:132
  21.8 3.0 copy-start.10
  28.0 3.6 slice-start
  28.0 3.6 slice-start.1
  34.9 29.7 %all-to-all-start = ((bf16[1,4,64,1920]{3,1,0,2:T(4,128)(2,1)}), bf16[1,4,64,1920]{3,1,0,2:T(4,128)(2,1)S(1)}, u32[]{:S(2)}, u32[]{:S(2)}) async-start(bf16[1,4,64,1920]{3,1,0,2:T(4,128)(2,1)} %copy.83), calls=%async_computation | async-start | bytes 1966080 | tf_op jit(solution)/shard_map/all_to_all | solution.py:123
  68.9 6.1 %copy-start.2 = (bf16[32,8,10,64]{3,2,1,0:T(8,128)(2,1)}, bf16[32,8,10,64]{3,2,1,0:T(8,128)(2,1)S(1)}, u32[]{:S(2)}) copy-start(bf16[32,8,10,64]{3,2,1,0:T(8,128)(2,1)S(1)} %reshape.164) | copy-start | bytes 983044
  80.4 13.9 %all-to-all-start.3 = ((bf16[1,32,8,640]{3,2,0,1:T(8,128)(2,1)}), bf16[1,32,8,640]{3,2,0,1:T(8,128)(2,1)S(1)}, u32[]{:S(2)}, u32[]{:S(2)}) async-start(bf16[1,32,8,640]{3,2,0,1:T(8,128)(2,1)} %bitcast.117), calls=%async_computation.4 | async-start | bytes 655360 | tf_op jit(solution)/shard_map/all_to_all | solution.py:126
  83.8 90.7 %reduce-scatter.8.cloned.1.call-start = ((), (), s32[]{:S(2)}) async-start(), calls=%async_computation.8 | async-start | bytes 1843200 | tf_op jit(solution)/shard_map/reduce_scatter | solution.py:169
  83.9 10.4 %copy-start.5 = (bf16[1,4,64,1280]{3,2,1,0:T(8,128)(2,1)S(1)}, bf16[1,4,64,1280]{3,2,1,0:T(8,128)(2,1)}, u32[]{:S(2)}) copy-start(bf16[1,4,64,1280]{3,2,1,0:T(8,128)(2,1)} %param.9) | copy-start | bytes 1966084
  96.2 1.2 copy-start.12
  96.2 173.0 %reduce-scatter.6.cloned.1.call-start = ((), (), s32[]{:S(2)}) async-start(), calls=%async_computation.7 | async-start | bytes 5529600 | tf_op jit(solution)/shard_map/reduce_scatter | solution.py:166
  97.4 2.8 copy-start.3
  100.2 0.8 copy-start.7
  148.0 293.6 %reduce-scatter.10.cloned.1.call-start = ((), (), s32[]{:S(2)}) async-start(), calls=%async_computation.10 | async-start | bytes 11059200 | tf_op jit(solution)/shard_map/reduce_scatter | solution.py:160
  148.3 4.2 copy-start.6
  153.0 1.1 copy-start.11
  154.1 1.1 copy-start.9
  174.4 303.7 %all-reduce.3.cloned.1.call-start = ((), (), s32[]{:S(2)}) async-start(), calls=%async_computation.11 | async-start | bytes 1638400 | tf_op jit(solution)/shard_map/psum | solution.py:177
  269.3 249.0 %all-gather.3.cloned.1.call-start = ((), (), s32[]{:S(2)}) async-start(), calls=%async_computation.9 | async-start | bytes 6144000 | tf_op jit(solution)/shard_map/all_gather | solution.py:176
  441.7 7.9 %collective-permute-start.1 = (bf16[1,1,64,1280]{3,2,1,0:T(8,128)(2,1)S(1)}, bf16[1,1,64,1280]{3,2,1,0:T(8,128)(2,1)S(1)}, u32[]{:S(2)}, u32[]{:S(2)}) collective-permute-start(bf16[1,1,64,1280]{3,2,1,0:T(8,128)(2,1)S(1)} %slice.59), channel_id=1, source_target_pairs={{1,0},{2,1},{3,2},{4,3},{5,4},{6,5},{7,6},{9,8},{10,9},{11,10},{12... | collective-permute-start | bytes 491528 | tf_op jit(solution)/shard_map/ppermute | solution.py:15
  518.3 4.6 copy-start.1
Sparse Core Ops, SparseCore 0:
  96.4 71.1 reduce-scatter.7
  171.7 97.5 reduce-scatter.5
  272.9 168.6 reduce-scatter.9
  444.0 34.0 all-reduce.2
  479.5 38.7 all-gather.2
